TPU v7x, 512 devices: a whole 4x8x8 slice. The times are simulated.
512 devices in a mesh: dp: 16 (over z, core), seq: 32 (over x, y).
Axes of the slice: x: 4, y: 8, z: 8, core: 2. Of those that a mesh axis runs over, the one named last changes fastest.
Arguments:
- inputs: bfloat16 [16, 4096, 4096], P('dp', 'seq'), may hold values from -6 to 6
- out_grads: bfloat16 [16, 4096, 14336], P('dp', 'seq'), may hold values from -6 to 6
- valid: int32 [16, 4096], P('dp', 'seq'), may hold values 0 or 1
- doc_blocks: int32 [16, 4], P('dp'), may hold values from 1 to 16, 32 in all within a row
- doc_ids: int32 [64], replicated, may hold values from 0 to 63, each once
- proj_in: bfloat16 [4096, 64], P('seq'), may hold values from -0.09375 to 0.09375
- proj_out: bfloat16 [14336, 64], P('seq'), may hold values from -0.046875 to 0.046875
- test_grads: bfloat16 [1024, 4096], P('seq'), may hold values from -192 to 192
Outputs:
- scores: float32 [64, 1024], P(None, 'seq')
Inputs may be any that keep to these rules, and one draw needn't show every extreme that they name: `doc_blocks`: each group's lengths sum to 32; the largest is 16 in every group. `doc_ids`: every document number appears once.
All inputs are finite; a program needn't handle non-finite values. No bound on the sum of `valid` on one device may be relied on, other than what follows from the above.
Results may differ from a plain program's by a relative error of at most 0.0003.
Values may be sent and summed in bfloat16 or wider, within the bound.
A program may use at most 64 MiB of HBM per device.

v0:
```python
import jax
import jax.numpy as jnp
from jax import lax
from jax.sharding import PartitionSpec as P

PROJ_OUT = 64
FEAT = 4096
BLOCK = 128
DOC_GRP = 4


def per_device(inputs, out_grads, valid, doc_blocks, doc_ids, proj_in, proj_out, test_grads):
    tokens = inputs[0]
    outgrad = out_grads[0]
    slots = tokens.shape[0]
    columns = tokens
    px = jnp.dot(
        columns,
        lax.all_gather(proj_in, "seq", axis=0, tiled=True),
        preferred_element_type=jnp.float32,
    )
    columns = outgrad
    pg = jnp.dot(
        columns,
        lax.all_gather(proj_out, "seq", axis=0, tiled=True),
        preferred_element_type=jnp.float32,
    )
    ends = jnp.cumsum(doc_blocks[0])
    position = lax.axis_index("seq") * slots + jnp.arange(slots, dtype=jnp.int32)
    blk = position // BLOCK
    owner = jnp.sum((blk[:, None] >= ends[None, :]).astype(jnp.int32), axis=1)
    onehot = (
        (owner[:, None] == jnp.arange(DOC_GRP, dtype=jnp.int32)[None, :]) & (valid[0][:, None] == 1)
    ).astype(jnp.float32)
    weighted = (onehot[:, :, None] * pg[:, None, :]).reshape(slots, DOC_GRP * PROJ_OUT)
    partial_grads = jnp.dot(weighted.T, px, precision=lax.Precision.HIGHEST).reshape(DOC_GRP, FEAT)
    ndocs = DOC_GRP * lax.axis_size("dp")
    group_grads = lax.psum(partial_grads, "seq")
    doc_grads = lax.all_gather(group_grads, "dp", axis=0, tiled=True)
    gram = jnp.dot(doc_grads, doc_grads.T, precision=lax.Precision.HIGHEST)
    cross = jnp.dot(doc_grads, test_grads.astype(jnp.float32).T, precision=lax.Precision.HIGHEST)
    damp = 0.1 * jnp.trace(gram) / ndocs
    matrix = gram / ndocs + damp * jnp.eye(ndocs, dtype=jnp.float32)
    factor = jnp.linalg.cholesky(matrix)
    middle = lax.linalg.triangular_solve(factor, cross, left_side=True, lower=True)
    solved = lax.linalg.triangular_solve(
        factor, middle, left_side=True, lower=True, transpose_a=True
    )
    placing = (doc_ids[None, :] == jnp.arange(ndocs, dtype=jnp.int32)[:, None]).astype(jnp.float32)
    return jnp.dot(placing, solved, precision=lax.Precision.HIGHEST)


def solution(mesh):
    in_specs = (
        P("dp", "seq", None),
        P("dp", "seq", None),
        P("dp", "seq"),
        P("dp", None),
        P(),
        P("seq", None),
        P("seq", None),
        P("seq", None),
    )
    out_specs = P(None, "seq")
    return jax.shard_map(
        per_device, mesh=mesh, in_specs=in_specs, out_specs=out_specs, check_vma=False
    )
```

profile of v0, /device:TPU:1, one launch (start us, length us, event | category | flops | bytes accessed | tf_op | source)
XLA Modules:
  0.0 325.9 jit_solution(14330074124522014039)
XLA Ops:
  6.5 0.7 all-gather.5.cloned.1.call-update
  7.3 0.0 all-reduce.2.cloned.1.call-start
  7.3 0.8 reduce-window.8
  8.1 0.1 convert_reduce_fusion
  8.2 41.4 %all_gather.10 = bf16[4096,64]{0,1:T(8,128)(2,1)S(1)} all-gather(bf16[128,64]{0,1:T(8,128)(2,1)} %param.13), channel_id=1, replica_groups=mesh['dp'=16,'seq'=32] {'seq'}, dimensions={0}, use_global_device_ids=true | all-gather | bytes 540672 | tf_op jit(solution)/shard_map/all_gather | solution.py:19
  49.6 0.7 compare_bitcast_fusion
  50.3 0.5 fusion.2
  50.8 44.7 %all-gather.5.cloned.1.call-done = bf16[32,448,64]{1,2,0:T(8,128)(2,1)} async-done(((bf16[1,448,64]{1,2,0:T(8,128)(2,1)}), bf16[32,448,64]{1,2,0:T(8,128)(2,1)}) %all-gather.5.cloned.1.call-update) | async-done | bytes 1835024 | tf_op jit(solution)/shard_map/all_gather | solution.py:25
  95.6 2.8 copy.20
  98.3 3.4 %reshape.113 = bf16[14336,64]{0,1:T(8,128)(2,1)} reshape(bf16[32,448,64]{1,0,2:T(8,128)(2,1)S(1)} %copy.20) | data formatting | bytes 3670016
  101.7 4.0 %fusion = f32[128,64]{0,1:T(8,128)S(1)} fusion(bf16[14336,64]{0,1:T(8,128)(2,1)} %reshape.113, bf16[1,128,14336]{2,1,0:T(8,128)(2,1)} %param.9), kind=kOutput, calls=%fused_computation | convolution fusion | flops 234881024 | bytes 5537792 | tf_op jit(solution)/shard_map/dot_general | solution.py:23
  105.7 0.3 fusion.15
  106.0 0.7 reshape.111
  106.7 0.0 all-reduce.2.cloned.1.call-update
  106.7 0.0 all-gather.7.cloned.1.call-start
  106.8 147.6 %all-reduce.2.cloned.1.call-done = f32[4,4096]{1,0:T(4,128)} async-done(((f32[4,4096]{1,0:T(4,128)}), f32[4,4096]{1,0:T(4,128)}) %all-reduce.2.cloned.1.call-update) | async-done | bytes 65552 | tf_op jit(solution)/shard_map/psum | solution.py:38
  254.4 0.0 all-gather.7.cloned.1.call-update
  254.4 47.1 %all-gather.7.cloned.1.call-done = f32[16,4,4096]{2,1,0:T(4,128)} async-done(((f32[1,4,4096]{2,1,0:T(4,128)}), f32[16,4,4096]{2,1,0:T(4,128)}) %all-gather.7.cloned.1.call-update) | async-done | bytes 1048592 | tf_op jit(solution)/shard_map/all_gather | solution.py:39
  301.5 1.6 reshape.115
  303.1 1.6 select_reduce_fusion.1
  304.7 0.1 copy.22
  304.8 0.1 copy.23
  305.6 5.8 %cholesky.17 = f32[64,64]{1,0:T(8,128)S(1)} custom-call(f32[64,64]{1,0:T(8,128)S(1)} %fusion.10), custom_call_target="Cholesky" | custom-call | tf_op jit(solution)/shard_map/jit(cholesky)/cholesky | solution.py:44
  311.4 0.6 compare_reduce_fusion
  312.1 0.7 fusion.4
  312.8 4.9 %custom-call.8 = f32[1,64,64]{1,2,0:T(8,128)S(1)} custom-call(f32[1,64,64]{2,1,0:T(8,128)S(1)} %fusion.4), custom_call_target="InvertDiagBlocksLowerTriangular" | custom-call | tf_op jit(solution)/shard_map/triangular_solve | solution.py:46
  317.6 0.0 copy-done.1
  317.7 0.6 fusion.16
  318.3 0.1 fusion.7
  318.4 0.2 fusion.5
  318.6 0.0 copy-done.2
  318.6 0.8 fusion.11
  (11 shorter events, 0.1 us)
Async XLA Ops:
  6.5 43.8 %copy-start = (bf16[1,128,4096]{2,1,0:T(8,128)(2,1)S(1)}, bf16[1,128,4096]{2,1,0:T(8,128)(2,1)}, u32[]{:S(2)}) copy-start(bf16[1,128,4096]{2,1,0:T(8,128)(2,1)} %param.8) | copy-start | bytes 3145732
  6.5 89.0 %all-gather.5.cloned.1.call-start = ((), (), s32[]{:S(2)}) async-start(), calls=%async_computation.1 | async-start | bytes 2162688 | tf_op jit(solution)/shard_map/all_gather | solution.py:25
  7.3 247.2 %all-reduce.2.cloned.1.call-start = ((), (), s32[]{:S(2)}) async-start(), calls=%async_computation | async-start | bytes 131072 | tf_op jit(solution)/shard_map/psum | solution.py:38
  106.7 194.8 %all-gather.7.cloned.1.call-start = ((), (), s32[]{:S(2)}) async-start(), calls=%async_computation.2 | async-start | bytes 1114112 | tf_op jit(solution)/shard_map/all_gather | solution.py:39
  254.4 63.2 %copy-start.1 = (bf16[32,4096]{1,0:T(8,128)(2,1)S(1)}, bf16[32,4096]{1,0:T(8,128)(2,1)}, u32[]{:S(2)}) copy-start(bf16[32,4096]{1,0:T(8,128)(2,1)} %param.15) | copy-start | bytes 786436
  303.1 15.5 %copy-start.2 = (s32[64]{0:T(128)S(1)}, s32[64]{0:T(128)}, u32[]{:S(2)}) copy-start(s32[64]{0:T(128)} %param.12) | copy-start | bytes 772
Sparse Core Ops, SparseCore 0:
  10.5 84.9 all-gather.4
  106.8 147.5 all-reduce.1
  256.5 44.9 all-gather.6
where the time goes:
time: 326 us
  waiting for transfers between devices  240 us (74%)
  blocking collectives  41.4 us (13%)
  between operations  13.9 us (4%)
  other arithmetic  13.7 us (4%)
  local copies, waits for them, and re-layouts  8.61 us (3%)
  matrix products  8 us (2%)
    psum x1, waiting for transfers between devices, per_device(): group_grads = lax.psum(partial_grads, 'seq')  148 us
    all_gather x1, waiting for transfers between devices, per_device(): doc_grads = lax.all_gather(group_grads, 'dp', axis=0, tiled=True)  47.1 us
    all_gather x1, waiting for transfers between devices, per_device(): lax.all_gather(proj_out, 'seq', axis=0, tiled=True)  44.7 us
    all_gather x1, blocking collectives, per_device(): lax.all_gather(proj_in, 'seq', axis=0, tiled=True)  41.4 us
  transfers between devices with their start and end apart: 3, of which 3 were waited for; matrix products, arithmetic and copies ran while one was open for 1% of the time, Pallas kernels for 0%

commit v1 on v0

--- a/solution.py
+++ b/solution.py
@@ -36,7 +36,12 @@
     partial_grads = jnp.dot(weighted.T, px, precision=lax.Precision.HIGHEST).reshape(DOC_GRP, FEAT)
     ndocs = DOC_GRP * lax.axis_size("dp")
     group_grads = lax.psum(partial_grads, "seq")
-    doc_grads = lax.all_gather(group_grads, "dp", axis=0, tiled=True)
+    ring = [group_grads]
+    for hop in range(15):
+        ring.append(lax.ppermute(ring[-1], "dp", [(dev, (dev + 1) % 16) for dev in range(16)]))
+    doc_grads = jnp.roll(
+        jnp.concatenate(ring[::-1], axis=0), (lax.axis_index("dp") + 1) * ring[0].shape[0], axis=0
+    )
     gram = jnp.dot(doc_grads, doc_grads.T, precision=lax.Precision.HIGHEST)
     cross = jnp.dot(doc_grads, test_grads.astype(jnp.float32).T, precision=lax.Precision.HIGHEST)
     damp = 0.1 * jnp.trace(gram) / ndocs

time: 326 us -> 372 us (1.14)
  local copies, waits for them, and re-layouts: 8.61 us -> 23.2 us
  waiting for transfers between devices: 240 us -> 254 us
  starting transfers between devices: 0.08 us -> 13 us
    ppermute x0 -> x15, waiting for transfers between devices: none -> 60.9 us  [per_device(): lax.ppermute(ring[-1], 'dp', [(dev, (dev + 1) % 16) for dev in range(16)])]
    all_gather x1 -> x0, waiting for transfers between devices: 47.1 us -> none  [per_device(): doc_grads = lax.all_gather(group_grads, 'dp', axis=0, tiled=True)]
    ppermute x0 -> x15, starting transfers between devices: none -> 12.9 us  [per_device(): lax.ppermute(ring[-1], 'dp', [(dev, (dev + 1) % 16) for dev in range(16)])]
    concatenate x0 -> x1, local copies, waits for them, and re-layouts: none -> 11.2 us  [per_device(): jnp.roll(jnp.concatenate(ring[::-1], axis=0), (lax.axis_index('dp') + 1)...]
    unnamed x8 -> x21, local copies, waits for them, and re-layouts: 4.99 us -> 8.42 us
  transfers between devices with their start and end apart: 3 -> 17, of which waited for: 3 -> 17; matrix products, arithmetic and copies ran while one was open for 1% -> 1% of each run, Pallas kernels for 0% -> 0%
where the time goes in v1:
time: 372 us; the launch traced here: 369 us
  waiting for transfers between devices  254 us (68%)
  blocking collectives  41.4 us (11%)
  local copies, waits for them, and re-layouts  23.2 us (6%)
  between operations  14.2 us (4%)
  other arithmetic  13.7 us (4%)
  starting transfers between devices  13 us (3%)
  matrix products  9.07 us (2%)
    psum x1, waiting for transfers between devices, per_device(): group_grads = lax.psum(partial_grads, 'seq')  148 us
    ppermute x15, waiting for transfers between devices, per_device(): lax.ppermute(ring[-1], 'dp', [(dev, (dev + 1) % 16) for dev in range(16)])  60.9 us
    all_gather x1, waiting for transfers between devices, per_device(): lax.all_gather(proj_out, 'seq', axis=0, tiled=True)  44.7 us
    all_gather x1, blocking collectives, per_device(): lax.all_gather(proj_in, 'seq', axis=0, tiled=True)  41.4 us
    ppermute x15, starting transfers between devices, per_device(): lax.ppermute(ring[-1], 'dp', [(dev, (dev + 1) % 16) for dev in range(16)])  12.9 us
    concatenate x1, local copies, waits for them, and re-layouts, per_device(): jnp.roll(jnp.concatenate(ring[::-1], axis=0), (lax.axis_index('dp') + 1)...  11.2 us
    unnamed x21, local copies, waits for them, and re-layouts  8.42 us
  transfers between devices with their start and end apart: 17, of which 17 were waited for; matrix products, arithmetic and copies ran while one was open for 1% of the time, Pallas kernels for 0%

profile of v1, /device:TPU:1, one launch (start us, length us, event | category | flops | bytes accessed | tf_op | source)
XLA Modules:
  0.0 368.6 jit_solution(16707502477458748978)
XLA Ops:
  7.3 0.8 reduce-window.8
  8.2 41.4 %all_gather.7 = bf16[4096,64]{0,1:T(8,128)(2,1)S(1)} all-gather(bf16[128,64]{0,1:T(8,128)(2,1)} %param.13), channel_id=1, replica_groups=mesh['dp'=16,'seq'=32] {'seq'}, dimensions={0}, use_global_device_ids=true | all-gather | bytes 540672 | tf_op jit(solution)/shard_map/all_gather | solution.py:19
  50.8 44.7 %all-gather.3.cloned.1.call-done = bf16[32,448,64]{1,2,0:T(8,128)(2,1)} async-done(((bf16[1,448,64]{1,2,0:T(8,128)(2,1)}), bf16[32,448,64]{1,2,0:T(8,128)(2,1)}) %all-gather.3.cloned.1.call-update) | async-done | bytes 1835024 | tf_op jit(solution)/shard_map/all_gather | solution.py:25
  95.6 2.8 copy.20
  98.3 3.4 reshape.113
  101.7 4.0 %fusion = f32[128,64]{0,1:T(8,128)S(1)} fusion(bf16[14336,64]{0,1:T(8,128)(2,1)} %reshape.113, bf16[1,128,14336]{2,1,0:T(8,128)(2,1)} %param.9), kind=kOutput, calls=%fused_computation | convolution fusion | flops 234881024 | bytes 5537792 | tf_op jit(solution)/shard_map/dot_general | solution.py:23
  106.8 147.7 %all-reduce.2.cloned.1.call-done = f32[4,4096]{1,0:T(4,128)} async-done(((f32[4,4096]{1,0:T(4,128)}), f32[4,4096]{1,0:T(4,128)}) %all-reduce.2.cloned.1.call-update) | async-done | bytes 65552 | tf_op jit(solution)/shard_map/psum | solution.py:38
  254.5 5.9 %collective-permute-start = (f32[4,4096]{1,0:T(4,128)}, f32[4,4096]{1,0:T(4,128)S(1)}, u32[]{:S(2)}, u32[]{:S(2)}) collective-permute-start(f32[4,4096]{1,0:T(4,128)} %all-reduce.2.cloned.1.call-done), channel_id=1, source_target_pairs={{0,32},{32,64},{64,96},{96,128},{128,160},{160,192},{192,224},{224... | collective-permute-start | bytes 196616 | tf_op jit(solution)/shard_map/ppermute | solution.py:41
  260.4 1.6 collective-permute-done
  262.1 2.3 collective-permute-start.1
  264.3 1.3 collective-permute-done.1
  265.6 2.4 collective-permute-start.2
  268.0 1.9 collective-permute-done.2
  269.9 1.8 collective-permute-start.3
  271.7 3.1 collective-permute-done.3
  275.4 4.3 %collective-permute-done.4 = f32[4,4096]{1,0:T(4,128)S(1)} collective-permute-done((f32[4,4096]{1,0:T(4,128)S(1)}, f32[4,4096]{1,0:T(4,128)S(1)}, u32[]{:S(2)}, u32[]{:S(2)}) %collective-permute-start.4) | collective-permute-done | bytes 65568 | tf_op jit(solution)/shard_map/ppermute | solution.py:41
  279.7 4.9 %collective-permute-done.5 = f32[4,4096]{1,0:T(4,128)S(1)} collective-permute-done((f32[4,4096]{1,0:T(4,128)S(1)}, f32[4,4096]{1,0:T(4,128)S(1)}, u32[]{:S(2)}, u32[]{:S(2)}) %collective-permute-start.5) | collective-permute-done | bytes 65568 | tf_op jit(solution)/shard_map/ppermute | solution.py:41
  284.6 4.9 %collective-permute-done.6 = f32[4,4096]{1,0:T(4,128)S(1)} collective-permute-done((f32[4,4096]{1,0:T(4,128)S(1)}, f32[4,4096]{1,0:T(4,128)S(1)}, u32[]{:S(2)}, u32[]{:S(2)}) %collective-permute-start.6) | collective-permute-done | bytes 65568 | tf_op jit(solution)/shard_map/ppermute | solution.py:41
  290.2 4.9 %collective-permute-done.7 = f32[4,4096]{1,0:T(4,128)S(1)} collective-permute-done((f32[4,4096]{1,0:T(4,128)S(1)}, f32[4,4096]{1,0:T(4,128)S(1)}, u32[]{:S(2)}, u32[]{:S(2)}) %collective-permute-start.7) | collective-permute-done | bytes 65568 | tf_op jit(solution)/shard_map/ppermute | solution.py:41
  295.7 4.9 %collective-permute-done.8 = f32[4,4096]{1,0:T(4,128)S(1)} collective-permute-done((f32[4,4096]{1,0:T(4,128)S(1)}, f32[4,4096]{1,0:T(4,128)S(1)}, u32[]{:S(2)}, u32[]{:S(2)}) %collective-permute-start.8) | collective-permute-done | bytes 65568 | tf_op jit(solution)/shard_map/ppermute | solution.py:41
  301.2 4.9 %collective-permute-done.9 = f32[4,4096]{1,0:T(4,128)S(1)} collective-permute-done((f32[4,4096]{1,0:T(4,128)S(1)}, f32[4,4096]{1,0:T(4,128)S(1)}, u32[]{:S(2)}, u32[]{:S(2)}) %collective-permute-start.9) | collective-permute-done | bytes 65568 | tf_op jit(solution)/shard_map/ppermute | solution.py:41
  306.7 4.9 %collective-permute-done.10 = f32[4,4096]{1,0:T(4,128)S(1)} collective-permute-done((f32[4,4096]{1,0:T(4,128)S(1)}, f32[4,4096]{1,0:T(4,128)S(1)}, u32[]{:S(2)}, u32[]{:S(2)}) %collective-permute-start.10) | collective-permute-done | bytes 65568 | tf_op jit(solution)/shard_map/ppermute | solution.py:41
  312.3 4.9 %collective-permute-done.11 = f32[4,4096]{1,0:T(4,128)S(1)} collective-permute-done((f32[4,4096]{1,0:T(4,128)S(1)}, f32[4,4096]{1,0:T(4,128)S(1)}, u32[]{:S(2)}, u32[]{:S(2)}) %collective-permute-start.11) | collective-permute-done | bytes 65568 | tf_op jit(solution)/shard_map/ppermute | solution.py:41
  317.8 4.9 %collective-permute-done.12 = f32[4,4096]{1,0:T(4,128)S(1)} collective-permute-done((f32[4,4096]{1,0:T(4,128)S(1)}, f32[4,4096]{1,0:T(4,128)S(1)}, u32[]{:S(2)}, u32[]{:S(2)}) %collective-permute-start.12) | collective-permute-done | bytes 65568 | tf_op jit(solution)/shard_map/ppermute | solution.py:41
  323.3 4.9 %collective-permute-done.13 = f32[4,4096]{1,0:T(4,128)S(1)} collective-permute-done((f32[4,4096]{1,0:T(4,128)S(1)}, f32[4,4096]{1,0:T(4,128)S(1)}, u32[]{:S(2)}, u32[]{:S(2)}) %collective-permute-start.13) | collective-permute-done | bytes 65568 | tf_op jit(solution)/shard_map/ppermute | solution.py:41
  328.8 4.4 %collective-permute-done.14 = f32[4,4096]{1,0:T(4,128)} collective-permute-done((f32[4,4096]{1,0:T(4,128)S(1)}, f32[4,4096]{1,0:T(4,128)}, u32[]{:S(2)}, u32[]{:S(2)}) %collective-permute-start.14) | collective-permute-done | bytes 65568 | tf_op jit(solution)/shard_map/ppermute | solution.py:41
  333.3 11.2 %concatenate.6 = f32[128,4096]{1,0:T(8,128)S(1)} concatenate(f32[4,4096]{1,0:T(4,128)} %collective-permute-done.14, f32[4,4096]{1,0:T(4,128)} %copy-done.8, f32[4,4096]{1,0:T(4,128)} %copy-done.7, f32[4,4096]{1,0:T(4,128)} %copy-done.6, f32[4,4096]{1,0:T(4,128)} %copy-done.5, f32[4,4096]{1,0:T(4,128)} %copy-done.4, f32[4,4096]{1,0:T(4,128)} %copy-done.3, f32[4,4096]{1,0:T(4,128)} %copy-done.2, ...), dimensions={0} | concatenate | bytes 4194304 | tf_op jit(solution)/shard_map/jit(_roll_dynamic)/concatenate | solution.py:42
  344.5 1.6 select_reduce_fusion.1
  346.1 1.6 fusion.4
  348.5 5.8 %cholesky.17 = f32[64,64]{1,0:T(8,128)S(1)} custom-call(f32[64,64]{1,0:T(8,128)S(1)} %fusion.14), custom_call_target="Cholesky" | custom-call | tf_op jit(solution)/shard_map/jit(cholesky)/cholesky | solution.py:49
  355.7 4.9 %custom-call.8 = f32[1,64,64]{1,2,0:T(8,128)S(1)} custom-call(f32[1,64,64]{2,1,0:T(8,128)S(1)} %fusion.8), custom_call_target="InvertDiagBlocksLowerTriangular" | custom-call | tf_op jit(solution)/shard_map/triangular_solve | solution.py:51
  361.0 0.8 fusion.15
  (52 shorter events, 10.5 us)
Async XLA Ops:
  6.5 43.8 %copy-start = (bf16[1,128,4096]{2,1,0:T(8,128)(2,1)S(1)}, bf16[1,128,4096]{2,1,0:T(8,128)(2,1)}, u32[]{:S(2)}) copy-start(bf16[1,128,4096]{2,1,0:T(8,128)(2,1)} %param.8) | copy-start | bytes 3145732
  6.5 89.0 %all-gather.3.cloned.1.call-start = ((), (), s32[]{:S(2)}) async-start(), calls=%async_computation.1 | async-start | bytes 2162688 | tf_op jit(solution)/shard_map/all_gather | solution.py:25
  7.3 247.2 %all-reduce.2.cloned.1.call-start = ((), (), s32[]{:S(2)}) async-start(), calls=%async_computation | async-start | bytes 131072 | tf_op jit(solution)/shard_map/psum | solution.py:38
  254.5 7.6 %collective-permute-start = (f32[4,4096]{1,0:T(4,128)}, f32[4,4096]{1,0:T(4,128)S(1)}, u32[]{:S(2)}, u32[]{:S(2)}) collective-permute-start(f32[4,4096]{1,0:T(4,128)} %all-reduce.2.cloned.1.call-done), channel_id=1, source_target_pairs={{0,32},{32,64},{64,96},{96,128},{128,160},{160,192},{192,224},{224... | collective-permute-start | bytes 196616 | tf_op jit(solution)/shard_map/ppermute | solution.py:41
  262.1 3.6 collective-permute-start.1
  265.6 4.3 %collective-permute-start.2 = (f32[4,4096]{1,0:T(4,128)S(1)}, f32[4,4096]{1,0:T(4,128)S(1)}, u32[]{:S(2)}, u32[]{:S(2)}) collective-permute-start(f32[4,4096]{1,0:T(4,128)S(1)} %collective-permute-done.1), channel_id=1, source_target_pairs={{0,32},{32,64},{64,96},{96,128},{128,160},{160,192},{192,224},{224... | collective-permute-start | bytes 196616 | tf_op jit(solution)/shard_map/ppermute | solution.py:41
  269.9 4.9 %collective-permute-start.3 = (f32[4,4096]{1,0:T(4,128)S(1)}, f32[4,4096]{1,0:T(4,128)S(1)}, u32[]{:S(2)}, u32[]{:S(2)}) collective-permute-start(f32[4,4096]{1,0:T(4,128)S(1)} %collective-permute-done.2), channel_id=1, source_target_pairs={{0,32},{32,64},{64,96},{96,128},{128,160},{160,192},{192,224},{224... | collective-permute-start | bytes 196616 | tf_op jit(solution)/shard_map/ppermute | solution.py:41
  274.8 4.9 %collective-permute-start.4 = (f32[4,4096]{1,0:T(4,128)S(1)}, f32[4,4096]{1,0:T(4,128)S(1)}, u32[]{:S(2)}, u32[]{:S(2)}) collective-permute-start(f32[4,4096]{1,0:T(4,128)S(1)} %collective-permute-done.3), channel_id=1, source_target_pairs={{0,32},{32,64},{64,96},{96,128},{128,160},{160,192},{192,224},{224... | collective-permute-start | bytes 196616 | tf_op jit(solution)/shard_map/ppermute | solution.py:41
  279.7 4.9 %collective-permute-start.5 = (f32[4,4096]{1,0:T(4,128)S(1)}, f32[4,4096]{1,0:T(4,128)S(1)}, u32[]{:S(2)}, u32[]{:S(2)}) collective-permute-start(f32[4,4096]{1,0:T(4,128)S(1)} %collective-permute-done.4), channel_id=1, source_target_pairs={{0,32},{32,64},{64,96},{96,128},{128,160},{160,192},{192,224},{224... | collective-permute-start | bytes 196616 | tf_op jit(solution)/shard_map/ppermute | solution.py:41
  284.6 4.9 %collective-permute-start.6 = (f32[4,4096]{1,0:T(4,128)S(1)}, f32[4,4096]{1,0:T(4,128)S(1)}, u32[]{:S(2)}, u32[]{:S(2)}) collective-permute-start(f32[4,4096]{1,0:T(4,128)S(1)} %collective-permute-done.5), channel_id=1, source_target_pairs={{0,32},{32,64},{64,96},{96,128},{128,160},{160,192},{192,224},{224... | collective-permute-start | bytes 196616 | tf_op jit(solution)/shard_map/ppermute | solution.py:41
  289.5 0.6 copy-start.1
  290.2 4.9 %collective-permute-start.7 = (f32[4,4096]{1,0:T(4,128)S(1)}, f32[4,4096]{1,0:T(4,128)S(1)}, u32[]{:S(2)}, u32[]{:S(2)}) collective-permute-start(f32[4,4096]{1,0:T(4,128)S(1)} %collective-permute-done.6), channel_id=1, source_target_pairs={{0,32},{32,64},{64,96},{96,128},{128,160},{160,192},{192,224},{224... | collective-permute-start | bytes 196616 | tf_op jit(solution)/shard_map/ppermute | solution.py:41
  295.1 0.6 copy-start.2
  295.7 4.9 %collective-permute-start.8 = (f32[4,4096]{1,0:T(4,128)S(1)}, f32[4,4096]{1,0:T(4,128)S(1)}, u32[]{:S(2)}, u32[]{:S(2)}) collective-permute-start(f32[4,4096]{1,0:T(4,128)S(1)} %collective-permute-done.7), channel_id=1, source_target_pairs={{0,32},{32,64},{64,96},{96,128},{128,160},{160,192},{192,224},{224... | collective-permute-start | bytes 196616 | tf_op jit(solution)/shard_map/ppermute | solution.py:41
  300.6 0.6 copy-start.3
  301.2 4.9 %collective-permute-start.9 = (f32[4,4096]{1,0:T(4,128)S(1)}, f32[4,4096]{1,0:T(4,128)S(1)}, u32[]{:S(2)}, u32[]{:S(2)}) collective-permute-start(f32[4,4096]{1,0:T(4,128)S(1)} %collective-permute-done.8), channel_id=1, source_target_pairs={{0,32},{32,64},{64,96},{96,128},{128,160},{160,192},{192,224},{224... | collective-permute-start | bytes 196616 | tf_op jit(solution)/shard_map/ppermute | solution.py:41
  306.1 0.6 copy-start.4
  306.7 4.9 %collective-permute-start.10 = (f32[4,4096]{1,0:T(4,128)S(1)}, f32[4,4096]{1,0:T(4,128)S(1)}, u32[]{:S(2)}, u32[]{:S(2)}) collective-permute-start(f32[4,4096]{1,0:T(4,128)S(1)} %collective-permute-done.9), channel_id=1, source_target_pairs={{0,32},{32,64},{64,96},{96,128},{128,160},{160,192},{192,224},{224... | collective-permute-start | bytes 196616 | tf_op jit(solution)/shard_map/ppermute | solution.py:41
  311.6 0.6 copy-start.5
  312.3 4.9 %collective-permute-start.11 = (f32[4,4096]{1,0:T(4,128)S(1)}, f32[4,4096]{1,0:T(4,128)S(1)}, u32[]{:S(2)}, u32[]{:S(2)}) collective-permute-start(f32[4,4096]{1,0:T(4,128)S(1)} %collective-permute-done.10), channel_id=1, source_target_pairs={{0,32},{32,64},{64,96},{96,128},{128,160},{160,192},{192,224},{224... | collective-permute-start | bytes 196616 | tf_op jit(solution)/shard_map/ppermute | solution.py:41
  317.2 0.6 copy-start.6
  317.8 4.9 %collective-permute-start.12 = (f32[4,4096]{1,0:T(4,128)S(1)}, f32[4,4096]{1,0:T(4,128)S(1)}, u32[]{:S(2)}, u32[]{:S(2)}) collective-permute-start(f32[4,4096]{1,0:T(4,128)S(1)} %collective-permute-done.11), channel_id=1, source_target_pairs={{0,32},{32,64},{64,96},{96,128},{128,160},{160,192},{192,224},{224... | collective-permute-start | bytes 196616 | tf_op jit(solution)/shard_map/ppermute | solution.py:41
  322.7 0.6 copy-start.7
  323.3 4.9 %collective-permute-start.13 = (f32[4,4096]{1,0:T(4,128)S(1)}, f32[4,4096]{1,0:T(4,128)S(1)}, u32[]{:S(2)}, u32[]{:S(2)}) collective-permute-start(f32[4,4096]{1,0:T(4,128)S(1)} %collective-permute-done.12), channel_id=1, source_target_pairs={{0,32},{32,64},{64,96},{96,128},{128,160},{160,192},{192,224},{224... | collective-permute-start | bytes 196616 | tf_op jit(solution)/shard_map/ppermute | solution.py:41
  328.2 0.6 copy-start.8
  328.2 5.0 %collective-permute-start.14 = (f32[4,4096]{1,0:T(4,128)S(1)}, f32[4,4096]{1,0:T(4,128)}, u32[]{:S(2)}, u32[]{:S(2)}) collective-permute-start(f32[4,4096]{1,0:T(4,128)S(1)} %collective-permute-done.13), channel_id=1, source_target_pairs={{0,32},{32,64},{64,96},{96,128},{128,160},{160,192},{192,224},{224... | collective-permute-start | bytes 196616 | tf_op jit(solution)/shard_map/ppermute | solution.py:41
  344.4 16.5 %copy-start.9 = (s32[64]{0:T(128)S(1)}, s32[64]{0:T(128)}, u32[]{:S(2)}) copy-start(s32[64]{0:T(128)} %param.12) | copy-start | bytes 772
Sparse Core Ops, SparseCore 0:
  10.5 84.9 all-gather.2
  106.9 147.5 all-reduce.1
